TPU v7x, 32 devices: a whole 2x2x4 slice. The times are simulated.
32 devices in a mesh: parts: 2 (over y), dp: 4 (over z), tensor: 4 (over x, core).
Axes of the slice: x: 2, y: 2, z: 4, core: 2. Of those that a mesh axis runs over, the one named last changes fastest.
Arguments:
- prompt_kv: bfloat16 [2, 14336, 8, 128], P(None, ('parts', 'dp'), 'tensor'), parts along dimension 1, may hold values from -12 to 12
- gen_kv: bfloat16 [64, 2, 128, 8, 128], P(('parts', 'dp'), None, None, 'tensor'), parts along dimension 0, may hold values from -17 to 17
- queries: bfloat16 [2, 64, 64, 128], P(None, ('parts', 'dp'), 'tensor'), parts along dimension 1, may hold values from -24 to 24
- new_kv: bfloat16 [2, 2, 64, 8, 128], P(None, None, ('parts', 'dp'), 'tensor'), parts along dimension 2, may hold values from -48 to 48
- ancestors: int32 [64], P(('parts', 'dp')), parts along dimension 0, may hold values from 0 to 31, as said below
- prior_twist: float32 [64], P(('parts', 'dp')), parts along dimension 0, may hold values from -290 to 6
- twist_vec: float32 [64, 128], P('tensor'), may hold values from -1 to 1
Outputs:
- attended: bfloat16 [2, 64, 64, 128], P(None, ('parts', 'dp'), 'tensor'), parts along dimension 1
- log_weights: float32 [64], P(('parts', 'dp')), parts along dimension 0
There are 2 independent parts, one for each index of `parts`. A program takes and returns all parts, laid end to end along the dimension named above; an argument that names none is the same for every part. Nothing has to cross between parts.
Inputs may be any that keep to these rules, and one draw needn't show every extreme that they name: Duplicates are allowed. Among the 8 particles of one device (equal p // 8) at most 4 have ancestors held by one same device (equal ancestors // 8), and every device has exactly 4 from some device.
All inputs are finite; a program needn't handle non-finite values.
Results may differ from a plain program's by a relative error of at most 0.0017.
Values may be sent and summed in bfloat16 or wider, within the bound.
A program may use at most 128 MiB of HBM per device.

v0:
```python
import math
import jax
import jax.numpy as jnp
from jax import lax
from jax.sharding import PartitionSpec as P


def join_states(left_state, right_state):
    largest = jnp.maximum(left_state[0], right_state[0])
    left_scale = jnp.exp(left_state[0] - largest)
    right_scale = jnp.exp(right_state[0] - largest)
    return (
        largest,
        left_state[1] * left_scale + right_state[1] * right_scale,
        left_state[2] * left_scale[..., None] + right_state[2] * right_scale[..., None],
    )


def fold_blocks(moments, totals, weighted, along):
    largest = jnp.max(moments, axis=along)
    scale_each = jnp.exp(moments - jnp.expand_dims(largest, along))
    return (
        largest,
        jnp.sum(totals * scale_each, axis=along),
        jnp.sum(weighted * scale_each[..., None], axis=along),
    )


def block_state(scores, values, pattern):
    largest = jnp.max(scores, axis=-1)
    exponent = jnp.exp(scores - largest[..., None])
    weighted = jnp.einsum(
        pattern, exponent.astype(jnp.bfloat16), values, preferred_element_type=jnp.float32
    )
    return (largest, jnp.sum(exponent, axis=-1), weighted)


def prompt_states(query_rows, prompt_kv, kv_count, scaling):
    row_count, head_count, head_size = query_rows.shape
    group_size = head_count // kv_count
    per_block = math.gcd(row_count, 256)
    blocked = query_rows.reshape(row_count // per_block, per_block, kv_count, group_size, head_size)
    key_rows = prompt_kv[0]
    values = prompt_kv[1]

    def attend_block(query_block):
        scores = (
            jnp.einsum("pcgd,kcd->pcgk", query_block, key_rows, preferred_element_type=jnp.float32)
            * scaling
        )
        return block_state(scores, values, "pcgk,kcd->pcgd")

    largest, totals, weighted = lax.map(attend_block, blocked)
    return (
        largest.reshape(row_count, head_count),
        totals.reshape(row_count, head_count),
        weighted.reshape(row_count, head_count, head_size),
    )


def per_device(prompt_kv, gen_kv, queries, new_kv, ancestors, prior_twist, twist_vec):
    step_count, local_count, head_count, head_size = queries.shape
    kv_count = prompt_kv.shape[2]
    group_size = head_count // kv_count
    scaling = 1.0 / math.sqrt(head_size)
    devices = lax.axis_size("dp")
    capacity = max(2, (2 * local_count + devices - 1) // devices)
    slot_total = devices * capacity
    source = ancestors // local_count
    offset = ancestors % local_count
    places = jnp.arange(local_count)
    earlier = (source[:, None] == source[None, :]) & (places[None, :] < places[:, None])
    arrival_rank = jnp.sum(earlier.astype(jnp.int32), axis=1)
    slot_index = source * capacity + arrival_rank
    slot_match = jnp.arange(slot_total)[:, None] == slot_index[None, :]
    wanted = jnp.sum(jnp.where(slot_match, offset[None, :] + 1, 0), axis=1) - 1
    requests_in = lax.all_to_all(
        wanted.reshape(devices, capacity), "dp", split_axis=0, concat_axis=0, tiled=True
    )
    picked = jnp.clip(requests_in, 0, local_count - 1).reshape(-1)
    every_prior = lax.all_gather(prior_twist, "dp", axis=0, tiled=True)
    twist_before = jnp.take(every_prior, ancestors, axis=0)
    split_query = queries.reshape(step_count, local_count, kv_count, group_size, head_size)
    sent_rows = jnp.take(gen_kv, picked, axis=0).reshape((devices, capacity) + gen_kv.shape[1:])
    arrived = lax.all_to_all(sent_rows, "dp", split_axis=0, concat_axis=0, tiled=True)
    resampled = jnp.take(arrived.reshape((slot_total,) + gen_kv.shape[1:]), slot_index, axis=0)
    cache_scores = (
        jnp.einsum(
            "spcgd,pkcd->spcgk", split_query, resampled[:, 0], preferred_element_type=jnp.float32
        )
        * scaling
    )
    largest, totals, weighted = block_state(cache_scores, resampled[:, 1], "spcgk,pkcd->spcgd")
    cached = (
        largest.reshape(step_count, local_count, head_count),
        totals.reshape(step_count, local_count, head_count),
        weighted.reshape(step_count, local_count, head_count, head_size),
    )
    new_scores = (
        jnp.einsum(
            "spcgd,tpcd->spcgt", split_query, new_kv[:, 0], preferred_element_type=jnp.float32
        )
        * scaling
    )
    positions = jnp.arange(step_count)
    allowed = positions[None, :] <= positions[:, None]
    new_scores = jnp.where(allowed[:, None, None, None, :], new_scores, -jnp.inf)
    largest, totals, weighted = block_state(new_scores, new_kv[:, 1], "spcgt,tpcd->spcgd")
    fresh_state = (
        largest.reshape(step_count, local_count, head_count),
        totals.reshape(step_count, local_count, head_count),
        weighted.reshape(step_count, local_count, head_count, head_size),
    )
    everyone = lax.all_gather(queries, "dp", axis=1, tiled=True)
    largest, totals, weighted = prompt_states(
        everyone.reshape(step_count * devices * local_count, head_count, head_size),
        prompt_kv,
        kv_count,
        scaling,
    )
    arrived_states = (
        lax.all_to_all(
            largest.reshape(step_count, devices, local_count, head_count),
            "dp",
            split_axis=1,
            concat_axis=1,
            tiled=True,
        ),
        lax.all_to_all(
            totals.reshape(step_count, devices, local_count, head_count),
            "dp",
            split_axis=1,
            concat_axis=1,
            tiled=True,
        ),
        lax.all_to_all(
            weighted.reshape(step_count, devices, local_count, head_count, head_size),
            "dp",
            split_axis=1,
            concat_axis=1,
            tiled=True,
        ),
    )
    prompt_state = fold_blocks(arrived_states[0], arrived_states[1], arrived_states[2], 1)
    joined = join_states(join_states(prompt_state, cached), fresh_state)
    attended = (joined[2] / joined[1][..., None]).astype(jnp.bfloat16)
    last_step = lax.optimization_barrier(attended[-1]).astype(jnp.float32)
    local_twist = jnp.sum(last_step * twist_vec, axis=(1, 2))
    twist_value = lax.psum(local_twist, "tensor")
    raw_weight = twist_value - twist_before
    largest_weight = lax.pmax(jnp.max(raw_weight), "dp")
    weight_mass = lax.psum(jnp.sum(jnp.exp(raw_weight - largest_weight)), "dp")
    normalizer = largest_weight + jnp.log(weight_mass)
    return (attended, raw_weight - normalizer)


def solution(mesh):
    placed = (
        P(None, ("parts", "dp"), "tensor", None),
        P(("parts", "dp"), None, None, "tensor", None),
        P(None, ("parts", "dp"), "tensor", None),
        P(None, None, ("parts", "dp"), "tensor", None),
        P(("parts", "dp")),
        P(("parts", "dp")),
        P("tensor", None),
    )
    return jax.shard_map(
        per_device,
        mesh=mesh,
        in_specs=placed,
        out_specs=(P(None, ("parts", "dp"), "tensor", None), P(("parts", "dp"))),
        check_vma=False,
    )
```

profile of v0, /device:TPU:0, one launch (start us, length us, event | category | flops | bytes accessed | tf_op | source)
XLA Modules:
  0.0 157.3 jit_solution(7130623179860953342)
XLA Ops:
  0.6 0.0 copy-start
  0.6 0.8 compare_select_fusion.3
  1.4 0.2 convert_reduce_fusion
  1.6 0.1 select_reduce_fusion
  1.7 0.7 sub.106
  2.4 6.3 %all-to-all-start.2 = ((s32[4,1,4]{2,1,0:T(1,128)}), s32[4,1,4]{2,1,0:T(1,128)S(1)}, u32[]{:S(2)}, u32[]{:S(2)}) async-start(s32[4,1,4]{2,1,0:T(1,128)} %bitcast.10), calls=%async_computation.2 | async-start | bytes 4096 | tf_op jit(solution)/shard_map/all_to_all | solution.py:77
  8.7 14.6 %all_gather.6 = bf16[2,32,16,128]{3,2,1,0:T(8,128)(2,1)S(1)} all-gather(bf16[2,8,16,128]{3,2,1,0:T(8,128)(2,1)} %param.9), channel_id=1, replica_groups=mesh['parts'=2,'dp'=4,'tensor'=4] {'dp'}, dimensions={1}, use_global_device_ids=true | all-gather | bytes 327680 | tf_op jit(solution)/shard_map/all_gather | solution.py:114
  23.4 0.1 copy.101
  23.4 2.5 %fusion.38 = (bf16[1,1792,2,128]{3,2,1,0:T(2,128)(2,1)S(1)}, bf16[1,1792,2,128]{3,2,1,0:T(2,128)(2,1)S(1)}) fusion(bf16[2,1792,2,128]{3,2,1,0:T(2,128)(2,1)} %param.7), kind=kLoop, calls=%fused_computation.88 | loop fusion | bytes 3670016 | tf_op jit(solution)/shard_map/slice | solution.py:44
  25.9 4.1 %bitcast_reduce_fusion = (f32[64,2,8]{0,2,1:T(8,128)S(1)}, f32[2,1792,64,8]{1,2,3,0:T(8,128)}) fusion(bf16[64,2,8,128]{3,0,2,1:T(8,128)(2,1)S(1)} %bitcast.113, bf16[1,1792,2,128]{3,2,1,0:T(2,128)(2,1)S(1)} %get-tuple-element.35), kind=kOutput, calls=%fused_computation.4 | convolution fusion | flops 473431040 | bytes 8523776 | tf_op jit(solution)/shard_map/while/body/eval_jaxpr/pcgd,kcd->pcgk/dot_general | solution.py:48
  30.0 0.1 reshape_reshape.11
  30.1 0.1 copy.105
  30.2 4.4 %fusion.3 = f32[2,64,8,128]{3,1,2,0:T(8,128)S(1)} fusion(f32[2,1792,64,8]{1,2,3,0:T(8,128)} %get-tuple-element.48, f32[64,2,8]{0,2,1:T(8,128)S(1)} %get-tuple-element.47, bf16[1,1792,2,128]{3,2,1,0:T(2,128)(2,1)S(1)} %get-tuple-element.34), kind=kOutput, calls=%fused_computation.8 | convolution fusion | flops 475267072 | bytes 8785920 | tf_op jit(solution)/shard_map/while/body/eval_jaxpr/pcgk,kcd->pcgd/dot_general | solution.py:32
  34.6 0.7 reshape.241
  35.3 0.0 all-to-all-done.2
  35.3 4.9 %all-to-all-start.1 = ((f32[4,1,256]{2,1,0:T(1,128)}), f32[4,1,256]{2,1,0:T(1,128)S(1)}, u32[]{:S(2)}, u32[]{:S(2)}) async-start(f32[4,1,256]{2,1,0:T(1,128)} %reshape.241), calls=%async_computation.1 | async-start | bytes 8192 | tf_op jit(solution)/shard_map/all_to_all | solution.py:122
  40.2 4.4 %fusion.1 = f32[64,2,8]{0,2,1:T(8,128)S(1)} fusion(f32[2,1792,64,8]{1,2,3,0:T(8,128)} %get-tuple-element.48, f32[64,2,8]{0,2,1:T(8,128)S(1)} %get-tuple-element.47), kind=kLoop, calls=%fused_computation.6 | loop fusion | flops 5504000 | bytes 7348224 | tf_op jit(solution)/shard_map/while/body/eval_jaxpr/reduce_sum | solution.py:35
  44.6 1.1 copy.104
  45.7 0.1 reshape_reshape.12
  45.8 0.1 copy.121
  45.9 0.7 reshape.243
  46.6 0.0 all-to-all-done.1
  46.6 5.1 %all-to-all-start.4 = ((f32[4,1,256]{2,1,0:T(1,128)}), f32[4,1,256]{2,1,0:T(1,128)S(1)}, u32[]{:S(2)}, u32[]{:S(2)}) async-start(f32[4,1,256]{2,1,0:T(1,128)} %reshape.243), calls=%async_computation.4 | async-start | bytes 8192 | tf_op jit(solution)/shard_map/all_to_all | solution.py:129
  51.7 0.1 min.18
  51.8 5.5 %all-to-all-done.4 = f32[4,1,256]{2,1,0:T(1,128)S(1)} async-done(((f32[4,1,256]{2,1,0:T(1,128)}), f32[4,1,256]{2,1,0:T(1,128)S(1)}, u32[]{:S(2)}, u32[]{:S(2)}) %all-to-all-start.4) | async-done | bytes 4128 | tf_op jit(solution)/shard_map/all_to_all | solution.py:129
  57.3 4.1 %all-to-all-start = ((f32[2,4,8,16,128]{4,3,2,0,1:T(8,128)}), f32[2,4,8,16,128]{4,3,2,0,1:T(8,128)}, u32[]{:S(2)}, u32[]{:S(2)}) async-start(f32[2,4,8,16,128]{4,3,2,0,1:T(8,128)} %copy.104), calls=%async_computation | async-start | bytes 1048576 | tf_op jit(solution)/shard_map/all_to_all | solution.py:136
  61.4 5.1 %gather_fusion = bf16[16,2,128,2,128]{4,3,2,1,0:T(2,128)(2,1)S(1)} fusion(bf16[8,2,128,2,128]{4,3,2,1,0:T(2,128)(2,1)S(1)} %copy-done, s32[1024]{0:T(1024)S(1)} %pad_clamp_fusion.2), kind=kCustom, calls=%fused_computation | custom fusion | bytes 4194368 | tf_op jit(solution)/shard_map/jit(_take)/gather | solution.py:84
  66.5 1.7 %copy_select_fusion = bf16[4,4,2,128,2,128]{5,3,4,2,1,0:T(8,128)(2,1)} fusion(bf16[4,4,2,128,2,128]{5,4,3,2,1,0:T(2,128)(2,1)S(1)} %bitcast.110, pred[4,4]{1,0:T(4,128)(4,1)S(1)} %compare_and_fusion), kind=kLoop, calls=%fused_computation.11 | loop fusion | flops 1048576 | bytes 4194320 | tf_op jit(solution)/shard_map/jit(_take)/select_n | solution.py:84
  68.2 3.6 %all-to-all-done = f32[2,4,8,16,128]{4,3,2,0,1:T(8,128)} async-done(((f32[2,4,8,16,128]{4,3,2,0,1:T(8,128)}), f32[2,4,8,16,128]{4,3,2,0,1:T(8,128)}, u32[]{:S(2)}, u32[]{:S(2)}) %all-to-all-start) | async-done | bytes 524320 | tf_op jit(solution)/shard_map/all_to_all | solution.py:136
  71.9 3.6 %all-to-all-start.3 = ((bf16[4,4,2,128,2,128]{5,3,4,2,1,0:T(8,128)(2,1)}), bf16[4,4,2,128,2,128]{5,3,4,2,1,0:T(8,128)(2,1)S(1)}, u32[]{:S(2)}, u32[]{:S(2)}) async-start(bf16[4,4,2,128,2,128]{5,3,4,2,1,0:T(8,128)(2,1)} %copy_select_fusion), calls=%async_computation.3 | async-start | bytes 4194304 | tf_op jit(solution)/shard_map/all_to_all | solution.py:85
  75.5 0.0 copy-done.3
  75.5 0.4 fusion.40
  76.0 0.1 fusion.22
  76.1 0.1 reshape.196
  76.1 0.1 reshape.193
  76.2 0.6 dynamic-slice
  77.5 0.2 dynamic-update-slice
  77.7 31.2 %all-reduce = f32[32]{0:T(128)S(1)} all-reduce(f32[32]{0:T(128)S(1)} %dynamic-update-slice), channel_id=1, replica_groups=mesh['parts'=2,'dp'=4,'tensor'=4] {'dp'}, use_global_device_ids=true, to_apply=%add | all-reduce | flops 32 | bytes 256
  109.0 0.2 convolution_bitcast_fusion.1
  109.2 0.5 broadcast.204
  109.7 0.7 reduce.4
  110.4 0.1 reshape.242
  110.4 0.7 reduce.5
  111.1 0.1 reshape.244
  111.2 1.3 multiply_reduce_fusion
  112.5 4.7 %all-to-all-done.3 = bf16[4,4,2,128,2,128]{5,3,4,2,1,0:T(8,128)(2,1)S(1)} async-done(((bf16[4,4,2,128,2,128]{5,3,4,2,1,0:T(8,128)(2,1)}), bf16[4,4,2,128,2,128]{5,3,4,2,1,0:T(8,128)(2,1)S(1)}, u32[]{:S(2)}, u32[]{:S(2)}) %all-to-all-start.3) | async-done | bytes 2097184 | tf_op jit(solution)/shard_map/all_to_all | solution.py:85
  117.2 1.7 %gather_fusion.1 = bf16[8,2,128,2,128]{4,2,3,1,0:T(8,128)(2,1)} fusion(bf16[16,2,128,2,128]{4,2,3,1,0:T(8,128)(2,1)S(1)} %bitcast.111, s32[1024]{0:T(1024)S(1)} %pad_clamp_fusion.1), kind=kCustom, calls=%fused_computation.1 | custom fusion | bytes 2097184 | tf_op jit(solution)/shard_map/jit(_take)/gather | solution.py:86
  118.9 1.4 copy_select_fusion.1
  120.3 0.5 fusion.41
  120.8 0.3 convolution_bitcast_fusion
  121.1 0.2 fusion.16
  121.3 0.1 reshape.191
  121.4 0.1 reshape.195
  121.5 0.2 fusion.13
  121.8 0.0 copy-start.1
  121.8 0.0 copy-done.4
  121.8 0.1 multiply_reduce_fusion.1
  121.9 0.6 gather_fusion.2
  122.6 5.7 %psum.14 = f32[8]{0:T(128)S(1)} all-reduce(f32[8]{0:T(128)S(1)} %multiply_reduce_fusion.1), channel_id=1, replica_groups=mesh['parts'=2,'dp'=4,'tensor'=4] {'tensor'}, use_global_device_ids=true, to_apply=%region_12.13 | all-reduce | flops 8 | bytes 64 | tf_op jit(solution)/shard_map/psum | solution.py:149
  128.2 0.6 fusion.34
  128.8 16.2 %pmax.7 = f32[]{:T(128)} all-reduce(f32[]{:T(128)} %get-tuple-element.16), channel_id=1, replica_groups=mesh['parts'=2,'dp'=4,'tensor'=4] {'dp'}, use_global_device_ids=true, to_apply=%region_14.15 | all-reduce | flops 1 | bytes 8 | tf_op jit(solution)/shard_map/pmax | solution.py:151
  145.0 1.3 exponential_reduce_fusion
  146.3 9.1 %psum.15 = f32[]{:T(128)} all-reduce(f32[]{:T(128)} %exponential_reduce_fusion), channel_id=1, replica_groups=mesh['parts'=2,'dp'=4,'tensor'=4] {'dp'}, use_global_device_ids=true, to_apply=%region_16.17 | all-reduce | flops 1 | bytes 8 | tf_op jit(solution)/shard_map/psum | solution.py:152
  156.8 0.5 broadcast_subtract_fusion
  (32 shorter events, 0.2 us)
Async XLA Ops:
  0.6 60.8 %copy-start = (bf16[8,2,128,2,128]{4,3,2,1,0:T(2,128)(2,1)S(1)}, bf16[8,2,128,2,128]{4,3,2,1,0:T(2,128)(2,1)}, u32[]{:S(2)}) copy-start(bf16[8,2,128,2,128]{4,3,2,1,0:T(2,128)(2,1)} %param.8) | copy-start | bytes 3145732
  2.4 32.9 %all-to-all-start.2 = ((s32[4,1,4]{2,1,0:T(1,128)}), s32[4,1,4]{2,1,0:T(1,128)S(1)}, u32[]{:S(2)}, u32[]{:S(2)}) async-start(s32[4,1,4]{2,1,0:T(1,128)} %bitcast.10), calls=%async_computation.2 | async-start | bytes 4096 | tf_op jit(solution)/shard_map/all_to_all | solution.py:77
  35.3 11.3 %all-to-all-start.1 = ((f32[4,1,256]{2,1,0:T(1,128)}), f32[4,1,256]{2,1,0:T(1,128)S(1)}, u32[]{:S(2)}, u32[]{:S(2)}) async-start(f32[4,1,256]{2,1,0:T(1,128)} %reshape.241), calls=%async_computation.1 | async-start | bytes 8192 | tf_op jit(solution)/shard_map/all_to_all | solution.py:122
  44.6 30.9 %copy-start.3 = (bf16[2,2,8,2,128]{4,3,2,1,0:T(2,128)(2,1)S(1)}, bf16[2,2,8,2,128]{4,3,2,1,0:T(2,128)(2,1)}, u32[]{:S(2)}) copy-start(bf16[2,2,8,2,128]{4,3,2,1,0:T(2,128)(2,1)} %param.10) | copy-start | bytes 49156
  44.6 30.9 %copy-start.2 = (bf16[2,8,16,128]{3,2,1,0:T(8,128)(2,1)S(1)}, bf16[2,8,16,128]{3,2,1,0:T(8,128)(2,1)}, u32[]{:S(2)}) copy-start(bf16[2,8,16,128]{3,2,1,0:T(8,128)(2,1)} %param.9) | copy-start | bytes 196612
  45.7 30.5 %copy-start.7 = (u32[32]{0:T(128)S(1)}, u32[32]{0:T(128)}, u32[]{:S(2)}) copy-start(u32[32]{0:T(128)} %constant.108) | copy-start | bytes 388
  45.7 31.8 %copy-start.6 = (f32[8]{0:T(128)S(1)}, f32[8]{0:T(128)}, u32[]{:S(2)}) copy-start(f32[8]{0:T(128)} %param.12) | copy-start | bytes 100
  46.6 10.7 %all-to-all-start.4 = ((f32[4,1,256]{2,1,0:T(1,128)}), f32[4,1,256]{2,1,0:T(1,128)S(1)}, u32[]{:S(2)}, u32[]{:S(2)}) async-start(f32[4,1,256]{2,1,0:T(1,128)} %reshape.243), calls=%async_computation.4 | async-start | bytes 8192 | tf_op jit(solution)/shard_map/all_to_all | solution.py:129
  57.3 14.6 %all-to-all-start = ((f32[2,4,8,16,128]{4,3,2,0,1:T(8,128)}), f32[2,4,8,16,128]{4,3,2,0,1:T(8,128)}, u32[]{:S(2)}, u32[]{:S(2)}) async-start(f32[2,4,8,16,128]{4,3,2,0,1:T(8,128)} %copy.104), calls=%async_computation | async-start | bytes 1048576 | tf_op jit(solution)/shard_map/all_to_all | solution.py:136
  68.2 53.6 %copy-start.4 = (f32[16,128]{1,0:T(8,128)S(1)}, f32[16,128]{1,0:T(8,128)}, u32[]{:S(2)}) copy-start(f32[16,128]{1,0:T(8,128)} %param.13) | copy-start | bytes 24580
  68.2 60.0 %copy-start.5 = (s32[8]{0:T(128)S(1)}, s32[8]{0:T(128)}, u32[]{:S(2)}) copy-start(s32[8]{0:T(128)} %param.11) | copy-start | bytes 100
  71.9 45.4 %all-to-all-start.3 = ((bf16[4,4,2,128,2,128]{5,3,4,2,1,0:T(8,128)(2,1)}), bf16[4,4,2,128,2,128]{5,3,4,2,1,0:T(8,128)(2,1)S(1)}, u32[]{:S(2)}, u32[]{:S(2)}) async-start(bf16[4,4,2,128,2,128]{5,3,4,2,1,0:T(8,128)(2,1)} %copy_select_fusion), calls=%async_computation.3 | async-start | bytes 4194304 | tf_op jit(solution)/shard_map/all_to_all | solution.py:85
  121.8 35.5 %copy-start.1 = (bf16[2,8,16,128]{3,2,1,0:T(8,128)(2,1)}, bf16[2,8,16,128]{3,2,1,0:T(8,128)(2,1)S(1)}, u32[]{:S(2)}) copy-start(bf16[2,8,16,128]{3,2,1,0:T(8,128)(2,1)S(1)} %fusion.13) | copy-start | bytes 196612
where the time goes:
time: 158 us; the launch traced here: 157 us
  blocking collectives  76.7 us (49%)
  starting transfers between devices  24 us (15%)
  local copies, waits for them, and re-layouts  15.5 us (10%)
  other arithmetic  14.3 us (9%)
  waiting for transfers between devices  13.8 us (9%)
  matrix products  9.94 us (6%)
  between operations  2.94 us (2%)
    unnamed x1, blocking collectives  31.2 us
    pmax x1, blocking collectives, per_device(): largest_weight = lax.pmax(jnp.max(raw_weight), 'dp')  16.2 us
    all_gather x1, blocking collectives, per_device(): everyone = lax.all_gather(queries, 'dp', axis=1, tiled=True)  14.6 us
    psum x1, blocking collectives, per_device(): weight_mass = lax.psum(jnp.sum(jnp.exp(raw_weight - largest_weight)), 'dp')  9.05 us
    all_to_all x1, starting transfers between devices, per_device(): lax.all_to_all(wanted.reshape(devices, capacity), 'dp', split_axis=0, con...  6.35 us
    psum x1, blocking collectives, per_device(): twist_value = lax.psum(local_twist, 'tensor')  5.66 us
    all_to_all x1, waiting for transfers between devices, per_device(): lax.all_to_all(totals.reshape(step_count, devices, local_count, head_coun...  5.47 us
    all_to_all x1, starting transfers between devices, per_device(): lax.all_to_all(totals.reshape(step_count, devices, local_count, head_coun...  5.09 us
  transfers between devices with their start and end apart: 5, of which 3 were waited for; matrix products, arithmetic and copies ran while one was open for 19% of the time, Pallas kernels for 0%

commit v1 on v0

--- a/solution.py
+++ b/solution.py
@@ -3,6 +3,29 @@
 import jax.numpy as jnp
 from jax import lax
 from jax.sharding import PartitionSpec as P
+
+
+def cut_along(x, dim, size):
+    lengths = x.shape
+    blocks = x.reshape(*lengths[:dim], size, lengths[dim] // size, *lengths[dim + 1 :])
+    return jnp.moveaxis(blocks, dim, 0)
+
+
+def in_order(blocks, dim):
+    blocks = jnp.moveaxis(blocks, 0, dim)
+    shape = blocks.shape
+    return blocks.reshape(*shape[:dim], shape[dim] * shape[dim + 1], *shape[dim + 2 :])
+
+
+def exchange_in_pairs(value, axis, split_dim, concat_dim):
+    size, here = (lax.axis_size(axis), lax.axis_index(axis))
+    parts = cut_along(value, split_dim, size)
+    finished = [parts[here]]
+    for step in range(1, size):
+        sent = parts[here ^ step]
+        finished.append(lax.ppermute(sent, axis, [(i, i ^ step) for i in range(size)]))
+    parts = jnp.stack(finished)[here ^ jnp.arange(size)]
+    return in_order(parts, concat_dim)
 
 
 def join_states(left_state, right_state):
@@ -126,13 +149,7 @@
             concat_axis=1,
             tiled=True,
         ),
-        lax.all_to_all(
-            totals.reshape(step_count, devices, local_count, head_count),
-            "dp",
-            split_axis=1,
-            concat_axis=1,
-            tiled=True,
-        ),
+        exchange_in_pairs(totals.reshape(step_count, devices, local_count, head_count), "dp", 1, 1),
         lax.all_to_all(
             weighted.reshape(step_count, devices, local_count, head_count, head_size),
             "dp",

time: 158 us -> 148 us (0.937)
  blocking collectives: 76.7 us -> 64.8 us
  waiting for transfers between devices: 13.8 us -> 17.3 us
    unnamed x1, blocking collectives: 31.2 us -> 22.8 us
    ppermute x0 -> x3, waiting for transfers between devices: none -> 8.38 us  [exchange_in_pairs(): lax.ppermute(sent, axis, [(i, i ^ step) for i in range(size)])]
    all_to_all x1 -> x0, waiting for transfers between devices: 5.47 us -> none  [per_device(): lax.all_to_all(totals.reshape(step_count, devices, local_count, head_coun...]
    all_to_all x1, waiting for transfers between devices: 0.01 us -> 5.47 us  [per_device(): lax.all_to_all(largest.reshape(step_count, devices, local_count, head_cou...]
    all_to_all x1 -> x0, starting transfers between devices: 5.09 us -> none  [per_device(): lax.all_to_all(totals.reshape(step_count, devices, local_count, head_coun...]
    all_to_all x1, waiting for transfers between devices: 4.73 us -> 0.01 us  [per_device(): lax.all_to_all(sent_rows, 'dp', split_axis=0, concat_axis=0, tiled=True)]
    ppermute x0 -> x3, starting transfers between devices: none -> 4.39 us  [exchange_in_pairs(): lax.ppermute(sent, axis, [(i, i ^ step) for i in range(size)])]
    pmax x1, blocking collectives: 16.2 us -> 12.7 us  [per_device(): largest_weight = lax.pmax(jnp.max(raw_weight), 'dp')]
  transfers between devices with their start and end apart: 5 -> 7, of which waited for: 3 -> 3; matrix products, arithmetic and copies ran while one was open for 19% -> 20% of each run, Pallas kernels for 0% -> 0%
where the time goes in v1:
time: 148 us
  blocking collectives  64.8 us (44%)
  starting transfers between devices  23.4 us (16%)
  waiting for transfers between devices  17.3 us (12%)
  local copies, waits for them, and re-layouts  15.5 us (10%)
  other arithmetic  13.7 us (9%)
  matrix products  9.95 us (7%)
  between operations  3.05 us (2%)
    unnamed x1, blocking collectives  22.8 us
    all_gather x1, blocking collectives, per_device(): everyone = lax.all_gather(queries, 'dp', axis=1, tiled=True)  14.6 us
    pmax x1, blocking collectives, per_device(): largest_weight = lax.pmax(jnp.max(raw_weight), 'dp')  12.7 us
    psum x1, blocking collectives, per_device(): weight_mass = lax.psum(jnp.sum(jnp.exp(raw_weight - largest_weight)), 'dp')  9.05 us
    ppermute x3, waiting for transfers between devices, exchange_in_pairs(): lax.ppermute(sent, axis, [(i, i ^ step) for i in range(size)])  8.38 us
    all_to_all x1, starting transfers between devices, per_device(): lax.all_to_all(wanted.reshape(devices, capacity), 'dp', split_axis=0, con...  6.35 us
    psum x1, blocking collectives, per_device(): twist_value = lax.psum(local_twist, 'tensor')  5.66 us
    all_to_all x1, waiting for transfers between devices, per_device(): lax.all_to_all(largest.reshape(step_count, devices, local_count, head_cou...  5.47 us
  transfers between devices with their start and end apart: 7, of which 3 were waited for; matrix products, arithmetic and copies ran while one was open for 20% of the time, Pallas kernels for 0%

profile of v1, /device:TPU:0, one launch (start us, length us, event | category | flops | bytes accessed | tf_op | source)
XLA Modules:
  0.0 147.7 jit_solution(11730348364155917473)
XLA Ops:
  0.6 0.0 copy-start
  0.6 0.8 compare_select_fusion.4
  1.4 0.2 convert_reduce_fusion
  1.6 0.1 select_reduce_fusion
  1.7 0.7 sub.106
  2.4 6.3 %all-to-all-start.2 = ((s32[4,1,4]{2,1,0:T(1,128)}), s32[4,1,4]{2,1,0:T(1,128)S(1)}, u32[]{:S(2)}, u32[]{:S(2)}) async-start(s32[4,1,4]{2,1,0:T(1,128)} %bitcast.10), calls=%async_computation.2 | async-start | bytes 4096 | tf_op jit(solution)/shard_map/all_to_all | solution.py:100
  8.7 14.6 %all_gather.6 = bf16[2,32,16,128]{3,2,1,0:T(8,128)(2,1)S(1)} all-gather(bf16[2,8,16,128]{3,2,1,0:T(8,128)(2,1)} %param.9), channel_id=1, replica_groups=mesh['parts'=2,'dp'=4,'tensor'=4] {'dp'}, dimensions={1}, use_global_device_ids=true | all-gather | bytes 327680 | tf_op jit(solution)/shard_map/all_gather | solution.py:137
  23.4 0.1 copy.85
  23.4 2.5 %fusion.40 = (bf16[1,1792,2,128]{3,2,1,0:T(2,128)(2,1)S(1)}, bf16[1,1792,2,128]{3,2,1,0:T(2,128)(2,1)S(1)}) fusion(bf16[2,1792,2,128]{3,2,1,0:T(2,128)(2,1)} %param.7), kind=kLoop, calls=%fused_computation.98 | loop fusion | bytes 3670016 | tf_op jit(solution)/shard_map/slice | solution.py:67
  25.9 4.1 %bitcast_reduce_fusion = (f32[64,2,8]{0,2,1:T(8,128)S(1)}, f32[2,1792,64,8]{1,2,3,0:T(8,128)}) fusion(bf16[64,2,8,128]{3,0,2,1:T(8,128)(2,1)S(1)} %bitcast.129, bf16[1,1792,2,128]{3,2,1,0:T(2,128)(2,1)S(1)} %get-tuple-element.35), kind=kOutput, calls=%fused_computation.5 | convolution fusion | flops 473431040 | bytes 8523776 | tf_op jit(solution)/shard_map/while/body/eval_jaxpr/pcgd,kcd->pcgk/dot_general | solution.py:71
  30.0 0.1 reshape_reshape.8
  30.1 4.4 %fusion.3 = f32[2,64,8,128]{3,1,2,0:T(8,128)S(1)} fusion(f32[2,1792,64,8]{1,2,3,0:T(8,128)} %get-tuple-element.52, f32[64,2,8]{0,2,1:T(8,128)S(1)} %get-tuple-element.51, bf16[1,1792,2,128]{3,2,1,0:T(2,128)(2,1)S(1)} %get-tuple-element.34), kind=kOutput, calls=%fused_computation.9 | convolution fusion | flops 475267072 | bytes 8785920 | tf_op jit(solution)/shard_map/while/body/eval_jaxpr/pcgk,kcd->pcgd/dot_general | solution.py:55
  34.5 1.1 copy.88
  35.6 0.1 copy.89
  35.7 0.7 reshape.278
  36.4 4.9 %all-to-all-start.1 = ((f32[4,1,256]{2,1,0:T(1,128)}), f32[4,1,256]{2,1,0:T(1,128)S(1)}, u32[]{:S(2)}, u32[]{:S(2)}) async-start(f32[4,1,256]{2,1,0:T(1,128)} %reshape.278), calls=%async_computation.1 | async-start | bytes 8192 | tf_op jit(solution)/shard_map/all_to_all | solution.py:145
  41.3 0.1 min.18
  41.4 5.5 %all-to-all-done.1 = f32[4,1,256]{2,1,0:T(1,128)S(1)} async-done(((f32[4,1,256]{2,1,0:T(1,128)}), f32[4,1,256]{2,1,0:T(1,128)S(1)}, u32[]{:S(2)}, u32[]{:S(2)}) %all-to-all-start.1) | async-done | bytes 4128 | tf_op jit(solution)/shard_map/all_to_all | solution.py:145
  46.9 4.1 %all-to-all-start = ((f32[2,4,8,16,128]{4,3,2,0,1:T(8,128)}), f32[2,4,8,16,128]{4,3,2,0,1:T(8,128)}, u32[]{:S(2)}, u32[]{:S(2)}) async-start(f32[2,4,8,16,128]{4,3,2,0,1:T(8,128)} %copy.88), calls=%async_computation | async-start | bytes 1048576 | tf_op jit(solution)/shard_map/all_to_all | solution.py:153
  51.1 5.1 %gather_fusion = bf16[16,2,128,2,128]{4,3,2,1,0:T(2,128)(2,1)S(1)} fusion(bf16[8,2,128,2,128]{4,3,2,1,0:T(2,128)(2,1)S(1)} %copy-done, s32[1024]{0:T(1024)S(1)} %pad_clamp_fusion.3), kind=kCustom, calls=%fused_computation | custom fusion | bytes 4194368 | tf_op jit(solution)/shard_map/jit(_take)/gather | solution.py:107
  56.2 0.0 copy-start.3
  56.2 1.7 %copy_select_fusion = bf16[4,4,2,128,2,128]{5,3,4,2,1,0:T(8,128)(2,1)} fusion(bf16[4,4,2,128,2,128]{5,4,3,2,1,0:T(2,128)(2,1)S(1)} %bitcast.126, pred[4,4]{1,0:T(4,128)(4,1)S(1)} %compare_and_fusion), kind=kLoop, calls=%fused_computation.12 | loop fusion | flops 1048576 | bytes 4194320 | tf_op jit(solution)/shard_map/jit(_take)/select_n | solution.py:107
  57.9 3.5 %all-to-all-done = f32[2,4,8,16,128]{4,3,2,0,1:T(8,128)} async-done(((f32[2,4,8,16,128]{4,3,2,0,1:T(8,128)}), f32[2,4,8,16,128]{4,3,2,0,1:T(8,128)}, u32[]{:S(2)}, u32[]{:S(2)}) %all-to-all-start) | async-done | bytes 524320 | tf_op jit(solution)/shard_map/all_to_all | solution.py:153
  61.4 3.6 %all-to-all-start.3 = ((bf16[4,4,2,128,2,128]{5,3,4,2,1,0:T(8,128)(2,1)}), bf16[4,4,2,128,2,128]{5,3,4,2,1,0:T(8,128)(2,1)S(1)}, u32[]{:S(2)}, u32[]{:S(2)}) async-start(bf16[4,4,2,128,2,128]{5,3,4,2,1,0:T(8,128)(2,1)} %copy_select_fusion), calls=%async_computation.3 | async-start | bytes 4194304 | tf_op jit(solution)/shard_map/all_to_all | solution.py:108
  65.0 4.4 %fusion.1 = f32[64,2,8]{0,2,1:T(8,128)S(1)} fusion(f32[2,1792,64,8]{1,2,3,0:T(8,128)} %get-tuple-element.52, f32[64,2,8]{0,2,1:T(8,128)S(1)} %get-tuple-element.51), kind=kLoop, calls=%fused_computation.7 | loop fusion | flops 5504000 | bytes 7348224 | tf_op jit(solution)/shard_map/while/body/eval_jaxpr/reduce_sum | solution.py:58
  69.5 0.1 reshape_reshape_reshape.3
  69.6 0.1 constant_dynamic-slice_fusion.3
  69.7 0.1 copy.102
  69.7 2.0 %collective-permute-start = (f32[2,1,8,16]{3,2,0,1:T(8,128)S(1)}, f32[2,1,8,16]{3,2,0,1:T(8,128)S(1)}, u32[]{:S(2)}, u32[]{:S(2)}) collective-permute-start(f32[2,1,8,16]{3,2,0,1:T(8,128)S(1)} %bitcast.132), channel_id=1, source_target_pairs={{0,4},{4,0},{8,12},{12,8},{1,5},{5,1},{9,13},{13,9},{2,6},{6,2},{1... | collective-permute-start | bytes 3080 | tf_op jit(solution)/shard_map/ppermute | solution.py:26
  71.7 0.1 copy.103
  71.8 2.4 %collective-permute-start.1 = (f32[2,1,8,16]{3,2,0,1:T(8,128)S(1)}, f32[2,1,8,16]{3,2,0,1:T(8,128)S(1)}, u32[]{:S(2)}, u32[]{:S(2)}) collective-permute-start(f32[2,1,8,16]{3,2,0,1:T(8,128)S(1)} %bitcast.133), channel_id=1, source_target_pairs={{0,8},{4,12},{8,0},{12,4},{1,9},{5,13},{9,1},{13,5},{2,10},{6,14},... | collective-permute-start | bytes 3080 | tf_op jit(solution)/shard_map/ppermute | solution.py:26
  74.1 0.1 copy.104
  74.2 0.1 collective-permute-start.2
  74.4 0.4 fusion.42
  74.8 0.1 fusion.23
  74.9 0.2 convolution_bitcast_fusion.1
  75.1 0.1 reshape.223
  75.2 0.1 reshape.219
  75.3 0.1 copy.101
  75.4 0.6 dynamic-slice.16
  76.6 0.2 dynamic-update-slice
  76.9 22.8 %all-reduce = f32[32]{0:T(128)S(1)} all-reduce(f32[32]{0:T(128)S(1)} %dynamic-update-slice), channel_id=1, replica_groups=mesh['parts'=2,'dp'=4,'tensor'=4] {'dp'}, use_global_device_ids=true, to_apply=%add | all-reduce | flops 32 | bytes 256
  99.7 8.4 %collective-permute-done.1 = f32[2,1,8,16]{3,2,0,1:T(8,128)S(1)} collective-permute-done((f32[2,1,8,16]{3,2,0,1:T(8,128)S(1)}, f32[2,1,8,16]{3,2,0,1:T(8,128)S(1)}, u32[]{:S(2)}, u32[]{:S(2)}) %collective-permute-start.1) | collective-permute-done | bytes 1056 | tf_op jit(solution)/shard_map/ppermute | solution.py:26
  108.0 0.6 gather_fusion.2
  108.6 0.5 broadcast.239
  109.1 0.7 reduce.4
  109.8 0.1 reshape.279
  109.9 1.3 multiply_reduce_fusion
  111.2 1.7 %gather_fusion.1 = bf16[8,2,128,2,128]{4,2,3,1,0:T(8,128)(2,1)} fusion(bf16[16,2,128,2,128]{4,2,3,1,0:T(8,128)(2,1)S(1)} %bitcast.127, s32[1024]{0:T(1024)S(1)} %pad_clamp_fusion.2), kind=kCustom, calls=%fused_computation.1 | custom fusion | bytes 2097184 | tf_op jit(solution)/shard_map/jit(_take)/gather | solution.py:109
  112.9 1.4 copy_select_fusion.1
  114.2 0.5 fusion.43
  114.7 0.3 convolution_bitcast_fusion
  115.0 0.2 fusion.16
  115.3 0.1 reshape.217
  115.4 0.1 reshape.222
  115.5 0.2 fusion.13
  115.7 0.1 multiply_reduce_fusion.1
  115.9 0.6 gather_fusion.3
  116.5 5.7 %psum.14 = f32[8]{0:T(128)S(1)} all-reduce(f32[8]{0:T(128)S(1)} %multiply_reduce_fusion.1), channel_id=1, replica_groups=mesh['parts'=2,'dp'=4,'tensor'=4] {'tensor'}, use_global_device_ids=true, to_apply=%region_12.13 | all-reduce | flops 8 | bytes 64 | tf_op jit(solution)/shard_map/psum | solution.py:166
  122.2 0.6 fusion.36
  122.8 12.7 %pmax.7 = f32[]{:T(128)} all-reduce(f32[]{:T(128)} %get-tuple-element.16), channel_id=1, replica_groups=mesh['parts'=2,'dp'=4,'tensor'=4] {'dp'}, use_global_device_ids=true, to_apply=%region_14.15 | all-reduce | flops 1 | bytes 8 | tf_op jit(solution)/shard_map/pmax | solution.py:168
  135.5 1.3 exponential_reduce_fusion
  136.8 9.1 %psum.15 = f32[]{:T(128)} all-reduce(f32[]{:T(128)} %exponential_reduce_fusion), channel_id=1, replica_groups=mesh['parts'=2,'dp'=4,'tensor'=4] {'dp'}, use_global_device_ids=true, to_apply=%region_16.17 | all-reduce | flops 1 | bytes 8 | tf_op jit(solution)/shard_map/psum | solution.py:169
  147.2 0.5 broadcast_subtract_fusion
  (41 shorter events, 0.3 us)
Async XLA Ops:
  0.6 50.4 %copy-start = (bf16[8,2,128,2,128]{4,3,2,1,0:T(2,128)(2,1)S(1)}, bf16[8,2,128,2,128]{4,3,2,1,0:T(2,128)(2,1)}, u32[]{:S(2)}) copy-start(bf16[8,2,128,2,128]{4,3,2,1,0:T(2,128)(2,1)} %param.8) | copy-start | bytes 3145732
  2.4 34.1 %all-to-all-start.2 = ((s32[4,1,4]{2,1,0:T(1,128)}), s32[4,1,4]{2,1,0:T(1,128)S(1)}, u32[]{:S(2)}, u32[]{:S(2)}) async-start(s32[4,1,4]{2,1,0:T(1,128)} %bitcast.10), calls=%async_computation.2 | async-start | bytes 4096 | tf_op jit(solution)/shard_map/all_to_all | solution.py:100
  36.4 10.4 %all-to-all-start.1 = ((f32[4,1,256]{2,1,0:T(1,128)}), f32[4,1,256]{2,1,0:T(1,128)S(1)}, u32[]{:S(2)}, u32[]{:S(2)}) async-start(f32[4,1,256]{2,1,0:T(1,128)} %reshape.278), calls=%async_computation.1 | async-start | bytes 8192 | tf_op jit(solution)/shard_map/all_to_all | solution.py:145
  46.9 14.5 %all-to-all-start = ((f32[2,4,8,16,128]{4,3,2,0,1:T(8,128)}), f32[2,4,8,16,128]{4,3,2,0,1:T(8,128)}, u32[]{:S(2)}, u32[]{:S(2)}) async-start(f32[2,4,8,16,128]{4,3,2,0,1:T(8,128)} %copy.88), calls=%async_computation | async-start | bytes 1048576 | tf_op jit(solution)/shard_map/all_to_all | solution.py:153
  56.2 18.2 %copy-start.3 = (bf16[2,2,8,2,128]{4,3,2,1,0:T(2,128)(2,1)S(1)}, bf16[2,2,8,2,128]{4,3,2,1,0:T(2,128)(2,1)}, u32[]{:S(2)}) copy-start(bf16[2,2,8,2,128]{4,3,2,1,0:T(2,128)(2,1)} %param.10) | copy-start | bytes 49156
  56.2 18.2 %copy-start.2 = (bf16[2,8,16,128]{3,2,1,0:T(8,128)(2,1)S(1)}, bf16[2,8,16,128]{3,2,1,0:T(8,128)(2,1)}, u32[]{:S(2)}) copy-start(bf16[2,8,16,128]{3,2,1,0:T(8,128)(2,1)} %param.9) | copy-start | bytes 196612
  57.9 17.5 %copy-start.7 = (u32[32]{0:T(128)S(1)}, u32[32]{0:T(128)}, u32[]{:S(2)}) copy-start(u32[32]{0:T(128)} %constant.120) | copy-start | bytes 388
  57.9 18.8 %copy-start.6 = (f32[8]{0:T(128)S(1)}, f32[8]{0:T(128)}, u32[]{:S(2)}) copy-start(f32[8]{0:T(128)} %param.12) | copy-start | bytes 100
  61.4 49.8 %all-to-all-start.3 = ((bf16[4,4,2,128,2,128]{5,3,4,2,1,0:T(8,128)(2,1)}), bf16[4,4,2,128,2,128]{5,3,4,2,1,0:T(8,128)(2,1)S(1)}, u32[]{:S(2)}, u32[]{:S(2)}) async-start(bf16[4,4,2,128,2,128]{5,3,4,2,1,0:T(8,128)(2,1)} %copy_select_fusion), calls=%async_computation.3 | async-start | bytes 4194304 | tf_op jit(solution)/shard_map/all_to_all | solution.py:108
  65.0 50.7 %copy-start.4 = (f32[16,128]{1,0:T(8,128)S(1)}, f32[16,128]{1,0:T(8,128)}, u32[]{:S(2)}) copy-start(f32[16,128]{1,0:T(8,128)} %param.13) | copy-start | bytes 24580
  65.0 57.2 %copy-start.5 = (s32[8]{0:T(128)S(1)}, s32[8]{0:T(128)}, u32[]{:S(2)}) copy-start(s32[8]{0:T(128)} %param.11) | copy-start | bytes 100
  69.7 29.9 %collective-permute-start = (f32[2,1,8,16]{3,2,0,1:T(8,128)S(1)}, f32[2,1,8,16]{3,2,0,1:T(8,128)S(1)}, u32[]{:S(2)}, u32[]{:S(2)}) collective-permute-start(f32[2,1,8,16]{3,2,0,1:T(8,128)S(1)} %bitcast.132), channel_id=1, source_target_pairs={{0,4},{4,0},{8,12},{12,8},{1,5},{5,1},{9,13},{13,9},{2,6},{6,2},{1... | collective-permute-start | bytes 3080 | tf_op jit(solution)/shard_map/ppermute | solution.py:26
  71.8 36.3 %collective-permute-start.1 = (f32[2,1,8,16]{3,2,0,1:T(8,128)S(1)}, f32[2,1,8,16]{3,2,0,1:T(8,128)S(1)}, u32[]{:S(2)}, u32[]{:S(2)}) collective-permute-start(f32[2,1,8,16]{3,2,0,1:T(8,128)S(1)} %bitcast.133), channel_id=1, source_target_pairs={{0,8},{4,12},{8,0},{12,4},{1,9},{5,13},{9,1},{13,5},{2,10},{6,14},... | collective-permute-start | bytes 3080 | tf_op jit(solution)/shard_map/ppermute | solution.py:26
  74.2 33.8 %collective-permute-start.2 = (f32[2,1,8,16]{3,2,0,1:T(8,128)S(1)}, f32[2,1,8,16]{3,2,0,1:T(8,128)S(1)}, u32[]{:S(2)}, u32[]{:S(2)}) collective-permute-start(f32[2,1,8,16]{3,2,0,1:T(8,128)S(1)} %bitcast.134), channel_id=1, source_target_pairs={{0,12},{4,8},{8,4},{12,0},{1,13},{5,9},{9,5},{13,1},{2,14},{6,10},... | collective-permute-start | bytes 3080 | tf_op jit(solution)/shard_map/ppermute | solution.py:26
  115.7 32.0 %copy-start.1 = (bf16[2,8,16,128]{3,2,1,0:T(8,128)(2,1)}, bf16[2,8,16,128]{3,2,1,0:T(8,128)(2,1)S(1)}, u32[]{:S(2)}) copy-start(bf16[2,8,16,128]{3,2,1,0:T(8,128)(2,1)S(1)} %fusion.13) | copy-start | bytes 196612
